TPU v7x, 512 devices: a whole 4x4x16 slice. The times are simulated.
512 devices in a mesh: ctx: 16 (over y, x_hi, core), fsdp: 32 (over z, x_lo).
Axes of the slice: x: 4 (x_hi: 2, x_lo: 2; x = x_hi * 2 + x_lo), y: 4, z: 16, core: 2. Of those that a mesh axis runs over, the one named last changes fastest.
Arguments:
- query_states: bfloat16 [32, 2048, 2048], P('fsdp', 'ctx'), may hold values from -12 to 12
- key_states: bfloat16 [32, 2048, 512], P('fsdp', 'ctx'), may hold values from -24 to 24
- value_states: bfloat16 [32, 2048, 512], P('fsdp', 'ctx'), may hold values from -170 to 170
- doc_ids: int32 [32, 2048], P('fsdp', 'ctx'), may hold values from 0 to 7, never falling along the last dimension, each value on 1 to 1536 neighbouring positions
- routes: int32 [32, 2048, 2], P('fsdp', 'ctx'), may hold values from 0 to 7, as said below
- route_weight: bfloat16 [32, 2048, 2], P('fsdp', 'ctx'), may hold values from 0.19921875 to 1
- cotangent: bfloat16 [32, 2048, 2048], P('fsdp', 'ctx'), may hold values from -6 to 6
- gate_weight: bfloat16 [2048, 7168], P('fsdp', 'ctx'), may hold values from -0.125 to 0.125
- up_weight: bfloat16 [2048, 7168], P('fsdp', 'ctx'), may hold values from -0.125 to 0.125
- down_weight: bfloat16 [7168, 2048], P('ctx', 'fsdp'), may hold values from -0.0625 to 0.0625
Outputs:
- attn_out: bfloat16 [32, 2048, 2048], P('fsdp', 'ctx')
- d_input: bfloat16 [32, 2048, 2048], P('fsdp', 'ctx')
Inputs may be any that keep to these rules, and one draw needn't show every extreme that they name: `routes`: each token names 2 different experts. Of the 128 tokens of one block of a sequence, at most 8 name expert 0; in some sequence every block has exactly 8 such tokens.
All inputs are finite; a program needn't handle non-finite values.
Results may differ from a plain program's by a relative error of at most 0.02.
Values may be sent and summed in bfloat16 or wider, within the bound.
No kernel may reach another device: no remote copies, remote signals or barrier semaphores. Data moves between devices by JAX's collectives and lax.ppermute only.
A program may use at most 64 MiB of HBM per device.

v0:
```python
import jax
import jax.numpy as jnp
from jax import lax
from jax.sharding import PartitionSpec as P

HEADS = 16
KV_HEADS = 4
HEAD_DIM = 128
CAP = 8
epsilon = 1e-05
far_below = -1e30


def from_behind(shard, axis, by):
    length = lax.axis_size(axis)
    return lax.ppermute(shard, axis, [(i, (i + by) % length) for i in range(length)])


def on_device(
    query_states,
    key_states,
    value_states,
    doc_ids,
    routes,
    route_weight,
    cotangent,
    gate_weight,
    up_weight,
    down_weight,
):
    gate_panel, up_panel, down_panel = (
        lax.all_gather(gate_weight, "fsdp", axis=0, tiled=True),
        lax.all_gather(up_weight, "fsdp", axis=0, tiled=True),
        lax.all_gather(down_weight, "fsdp", axis=1, tiled=True),
    )
    every_doc = lax.all_gather(doc_ids, "ctx", axis=1, tiled=True)[0]
    cycle_size = lax.axis_size("ctx")
    position = lax.axis_index("ctx")
    tok_count = query_states.shape[1]
    model_width = query_states.shape[2]
    group_size = HEADS // KV_HEADS
    scaling = HEAD_DIM ** (-0.5)
    query_heads = query_states[0].reshape(tok_count, KV_HEADS, group_size, HEAD_DIM)
    query_docs = lax.dynamic_slice_in_dim(every_doc, position * tok_count, tok_count)

    def attend_block(running, key_block, source):
        key_heads = key_block[0].reshape(tok_count, KV_HEADS, HEAD_DIM)
        value_heads = key_block[1].reshape(tok_count, KV_HEADS, HEAD_DIM)
        key_docs = lax.dynamic_slice_in_dim(every_doc, source * tok_count, tok_count)
        allowed = key_docs[None, :] == query_docs[:, None]
        row_max, row_total, weighted = running
        scores = (
            jnp.einsum("igrd,jgd->grij", query_heads, key_heads, preferred_element_type=jnp.float32)
            * scaling
        )
        masked = jnp.where(allowed, scores, far_below)
        new_max = jnp.maximum(row_max, jnp.max(masked, axis=-1))
        unscaled = jnp.where(allowed, jnp.exp(masked - new_max[..., None]), 0.0)
        factor = jnp.exp(row_max - new_max)
        probabilities = unscaled.astype(jnp.bfloat16)
        weighted = weighted * factor[..., None] + jnp.einsum(
            "grij,jgd->grid", probabilities, value_heads, preferred_element_type=jnp.float32
        )
        return (new_max, row_total * factor + jnp.sum(unscaled, axis=-1), weighted)

    own_block = (key_states[0], value_states[0])
    start_state = (
        jnp.full((KV_HEADS, group_size, tok_count), far_below, jnp.float32),
        jnp.zeros((KV_HEADS, group_size, tok_count), jnp.float32),
        jnp.zeros((KV_HEADS, group_size, tok_count, HEAD_DIM), jnp.float32),
    )
    running = attend_block(start_state, own_block, position)

    def cycle_step(step_index, loop_state):
        running_now, key_block = loop_state
        key_block = from_behind((key_block[0], key_block[1]), "ctx", 1)
        return (
            attend_block(running_now, key_block, (position - step_index) % cycle_size),
            key_block,
        )

    running, last_block = lax.fori_loop(1, cycle_size, cycle_step, (running, own_block))
    row_max, row_total, weighted = running
    mixed = weighted / row_total[..., None]
    attn_out = (
        jnp.transpose(mixed, (2, 0, 1, 3)).reshape(tok_count, model_width).astype(jnp.bfloat16)
    )
    as_float = attn_out.astype(jnp.float32)
    inverse = lax.rsqrt(jnp.mean(as_float * as_float, axis=-1, keepdims=True) + epsilon)
    scaled = as_float * inverse
    normed = scaled.astype(jnp.bfloat16)
    chosen = routes[0] == 0
    routed = jnp.any(chosen, axis=-1)
    weight = jnp.sum(jnp.where(chosen, route_weight[0].astype(jnp.float32), 0.0), axis=-1)
    slot_index = jnp.cumsum(routed.astype(jnp.int32)) - 1
    selector = (slot_index[None, :] == jnp.arange(CAP, dtype=jnp.int32)[:, None]) & routed[None, :]
    selector_half = selector.astype(jnp.bfloat16)
    selector_float = selector.astype(jnp.float32)
    slot_x = jnp.dot(selector_half, normed, preferred_element_type=jnp.float32).astype(jnp.bfloat16)
    slot_dy = jnp.dot(selector_half, cotangent[0], preferred_element_type=jnp.float32).astype(
        jnp.bfloat16
    )
    slot_w = jnp.dot(selector_float, weight, precision=lax.Precision.HIGHEST).astype(jnp.bfloat16)
    rows_x, rows_dy, rows_w = (
        lax.all_gather(slot_x, "ctx", axis=0, tiled=True),
        lax.all_gather(slot_dy, "ctx", axis=0, tiled=True),
        lax.all_gather(slot_w, "ctx", axis=0, tiled=True),
    )
    contract_last = (((1,), (1,)), ((), ()))
    gate_proj = jnp.dot(rows_x, gate_panel, preferred_element_type=jnp.float32)
    up_proj = jnp.dot(rows_x, up_panel, preferred_element_type=jnp.float32)
    back_grad = lax.dot_general(
        rows_dy, down_panel, contract_last, preferred_element_type=jnp.float32
    )
    back_grad = back_grad * rows_w.astype(jnp.float32)[:, None]
    sigmoid_gate = jax.nn.sigmoid(gate_proj)
    grad_gate = (
        back_grad * up_proj * sigmoid_gate * (1.0 + gate_proj * (1.0 - sigmoid_gate))
    ).astype(jnp.bfloat16)
    grad_up = (back_grad * gate_proj * sigmoid_gate).astype(jnp.bfloat16)
    result = lax.dot_general(
        grad_gate, gate_panel, contract_last, preferred_element_type=jnp.float32
    )
    d_slots = lax.psum_scatter(
        (
            result
            + lax.dot_general(grad_up, up_panel, contract_last, preferred_element_type=jnp.float32)
        ).astype(jnp.bfloat16),
        "ctx",
        scatter_dimension=0,
        tiled=True,
    ).astype(jnp.float32)
    d_norm = jnp.dot(selector_float.T, d_slots, precision=lax.Precision.HIGHEST)
    d_input = inverse * (d_norm - scaled * jnp.mean(d_norm * scaled, axis=-1, keepdims=True))
    return (attn_out[None], d_input.astype(jnp.bfloat16)[None])


def solution(mesh):
    return jax.shard_map(
        on_device,
        mesh=mesh,
        in_specs=(
            P("fsdp", "ctx", None),
            P("fsdp", "ctx", None),
            P("fsdp", "ctx", None),
            P("fsdp", "ctx"),
            P("fsdp", "ctx", None),
            P("fsdp", "ctx", None),
            P("fsdp", "ctx", None),
            P("fsdp", "ctx"),
            P("fsdp", "ctx"),
            P("ctx", "fsdp"),
        ),
        out_specs=(P("fsdp", "ctx", None), P("fsdp", "ctx", None)),
        check_vma=False,
    )
```

profile of v0, /device:TPU:32, one launch (start us, length us, event | category | flops | bytes accessed | tf_op | source)
XLA Modules:
  0.0 520.8 jit_solution(569136732008379769)
XLA Ops:
  13.4 24.6 %all_gather.21 = s32[1,2048]{1,0:T(1,128)S(1)} all-gather(s32[1,128]{1,0:T(1,128)} %param.15), channel_id=1, replica_groups=mesh['ctx'=16,'fsdp'=32] {'ctx'}, dimensions={1}, use_global_device_ids=true | all-gather | bytes 8704 | tf_op jit(solution)/shard_map/all_gather | solution.py:36
  40.8 206.7 %while.23 = (s32[]{:T(128)}, f32[4,4,128]{2,1,0:T(4,128)S(1)}, f32[4,4,128]{2,1,0:T(4,128)S(1)}, f32[4,4,128,128]{3,2,1,0:T(8,128)S(1)}, bf16[128,512]{0,1:T(8,1...) while((s32[]{:T(128)}, f32[4,4,128]{2,1,0:T(4,128)S(1)}, ...), condition=%wide.region_5.6_spmd, body=%wide.region_2.5_spmd.sunk | while | flops 137121808 | bytes 7801232 | solution.py:82
  40.9 2.3 collective-permute-start
  45.2 5.8 %collective-permute-done = bf16[128,512]{0,1:T(8,128)(2,1)S(1)} collective-permute-done((bf16[128,512]{0,1:T(8,128)(2,1)S(1)}, bf16[128,512]{0,1:T(8,128)(2,1)S(1)}, u32[]{:S(2)}, u32[]{:S(2)}) %collective-permute-start) | collective-permute-done | bytes 131104 | tf_op jit(solution)/shard_map/while/body/eval_jaxpr/ppermute | solution.py:16
  51.6 2.8 collective-permute-done.1
  59.2 7.0 %collective-permute-done = bf16[128,512]{0,1:T(8,128)(2,1)S(1)} collective-permute-done((bf16[128,512]{0,1:T(8,128)(2,1)S(1)}, bf16[128,512]{0,1:T(8,128)(2,1)S(1)}, u32[]{:S(2)}, u32[]{:S(2)}) %collective-permute-start) | collective-permute-done | bytes 131104 | tf_op jit(solution)/shard_map/while/body/eval_jaxpr/ppermute | solution.py:16
  73.5 7.0 %collective-permute-done = bf16[128,512]{0,1:T(8,128)(2,1)S(1)} collective-permute-done((bf16[128,512]{0,1:T(8,128)(2,1)S(1)}, bf16[128,512]{0,1:T(8,128)(2,1)S(1)}, u32[]{:S(2)}, u32[]{:S(2)}) %collective-permute-start) | collective-permute-done | bytes 131104 | tf_op jit(solution)/shard_map/while/body/eval_jaxpr/ppermute | solution.py:16
  87.4 7.3 %collective-permute-done = bf16[128,512]{0,1:T(8,128)(2,1)S(1)} collective-permute-done((bf16[128,512]{0,1:T(8,128)(2,1)S(1)}, bf16[128,512]{0,1:T(8,128)(2,1)S(1)}, u32[]{:S(2)}, u32[]{:S(2)}) %collective-permute-start) | collective-permute-done | bytes 131104 | tf_op jit(solution)/shard_map/while/body/eval_jaxpr/ppermute | solution.py:16
  101.4 7.2 %collective-permute-done = bf16[128,512]{0,1:T(8,128)(2,1)S(1)} collective-permute-done((bf16[128,512]{0,1:T(8,128)(2,1)S(1)}, bf16[128,512]{0,1:T(8,128)(2,1)S(1)}, u32[]{:S(2)}, u32[]{:S(2)}) %collective-permute-start) | collective-permute-done | bytes 131104 | tf_op jit(solution)/shard_map/while/body/eval_jaxpr/ppermute | solution.py:16
  115.8 6.4 %collective-permute-done = bf16[128,512]{0,1:T(8,128)(2,1)S(1)} collective-permute-done((bf16[128,512]{0,1:T(8,128)(2,1)S(1)}, bf16[128,512]{0,1:T(8,128)(2,1)S(1)}, u32[]{:S(2)}, u32[]{:S(2)}) %collective-permute-start) | collective-permute-done | bytes 131104 | tf_op jit(solution)/shard_map/while/body/eval_jaxpr/ppermute | solution.py:16
  122.8 2.1 collective-permute-done.1
  129.7 6.4 %collective-permute-done = bf16[128,512]{0,1:T(8,128)(2,1)S(1)} collective-permute-done((bf16[128,512]{0,1:T(8,128)(2,1)S(1)}, bf16[128,512]{0,1:T(8,128)(2,1)S(1)}, u32[]{:S(2)}, u32[]{:S(2)}) %collective-permute-start) | collective-permute-done | bytes 131104 | tf_op jit(solution)/shard_map/while/body/eval_jaxpr/ppermute | solution.py:16
  142.5 6.2 %collective-permute-done = bf16[128,512]{0,1:T(8,128)(2,1)S(1)} collective-permute-done((bf16[128,512]{0,1:T(8,128)(2,1)S(1)}, bf16[128,512]{0,1:T(8,128)(2,1)S(1)}, u32[]{:S(2)}, u32[]{:S(2)}) %collective-permute-start) | collective-permute-done | bytes 131104 | tf_op jit(solution)/shard_map/while/body/eval_jaxpr/ppermute | solution.py:16
  155.1 5.8 %collective-permute-done = bf16[128,512]{0,1:T(8,128)(2,1)S(1)} collective-permute-done((bf16[128,512]{0,1:T(8,128)(2,1)S(1)}, bf16[128,512]{0,1:T(8,128)(2,1)S(1)}, u32[]{:S(2)}, u32[]{:S(2)}) %collective-permute-start) | collective-permute-done | bytes 131104 | tf_op jit(solution)/shard_map/while/body/eval_jaxpr/ppermute | solution.py:16
  167.7 6.2 %collective-permute-done = bf16[128,512]{0,1:T(8,128)(2,1)S(1)} collective-permute-done((bf16[128,512]{0,1:T(8,128)(2,1)S(1)}, bf16[128,512]{0,1:T(8,128)(2,1)S(1)}, u32[]{:S(2)}, u32[]{:S(2)}) %collective-permute-start) | collective-permute-done | bytes 131104 | tf_op jit(solution)/shard_map/while/body/eval_jaxpr/ppermute | solution.py:16
  174.5 2.3 collective-permute-done.1
  181.6 7.0 %collective-permute-done = bf16[128,512]{0,1:T(8,128)(2,1)S(1)} collective-permute-done((bf16[128,512]{0,1:T(8,128)(2,1)S(1)}, bf16[128,512]{0,1:T(8,128)(2,1)S(1)}, u32[]{:S(2)}, u32[]{:S(2)}) %collective-permute-start) | collective-permute-done | bytes 131104 | tf_op jit(solution)/shard_map/while/body/eval_jaxpr/ppermute | solution.py:16
  195.6 7.1 %collective-permute-done = bf16[128,512]{0,1:T(8,128)(2,1)S(1)} collective-permute-done((bf16[128,512]{0,1:T(8,128)(2,1)S(1)}, bf16[128,512]{0,1:T(8,128)(2,1)S(1)}, u32[]{:S(2)}, u32[]{:S(2)}) %collective-permute-start) | collective-permute-done | bytes 131104 | tf_op jit(solution)/shard_map/while/body/eval_jaxpr/ppermute | solution.py:16
  209.9 6.8 %collective-permute-done = bf16[128,512]{0,1:T(8,128)(2,1)S(1)} collective-permute-done((bf16[128,512]{0,1:T(8,128)(2,1)S(1)}, bf16[128,512]{0,1:T(8,128)(2,1)S(1)}, u32[]{:S(2)}, u32[]{:S(2)}) %collective-permute-start) | collective-permute-done | bytes 131104 | tf_op jit(solution)/shard_map/while/body/eval_jaxpr/ppermute | solution.py:16
  223.9 6.3 %collective-permute-done = bf16[128,512]{0,1:T(8,128)(2,1)S(1)} collective-permute-done((bf16[128,512]{0,1:T(8,128)(2,1)S(1)}, bf16[128,512]{0,1:T(8,128)(2,1)S(1)}, u32[]{:S(2)}, u32[]{:S(2)}) %collective-permute-start) | collective-permute-done | bytes 131104 | tf_op jit(solution)/shard_map/while/body/eval_jaxpr/ppermute | solution.py:16
  230.8 2.1 collective-permute-done.1
  237.7 6.3 %collective-permute-done = bf16[128,512]{0,1:T(8,128)(2,1)S(1)} collective-permute-done((bf16[128,512]{0,1:T(8,128)(2,1)S(1)}, bf16[128,512]{0,1:T(8,128)(2,1)S(1)}, u32[]{:S(2)}, u32[]{:S(2)}) %collective-permute-start) | collective-permute-done | bytes 131104 | tf_op jit(solution)/shard_map/while/body/eval_jaxpr/ppermute | solution.py:16
  244.6 2.3 collective-permute-done.1
  254.2 33.2 %all-reduce = bf16[128]{0:T(256)(128)(2,1)S(1)} all-reduce(bf16[128]{0:T(256)(128)(2,1)S(1)} %dynamic-update-slice), channel_id=1, replica_groups=mesh['ctx'=16,'fsdp'=32] {'ctx'}, use_global_device_ids=true, to_apply=%add | all-reduce | flops 128 | bytes 512
  287.9 22.7 %all_gather.25 = bf16[128,2048]{1,0:T(8,128)(2,1)S(1)} all-gather(bf16[8,2048]{1,0:T(8,128)(2,1)S(1)} %convolution_convert_fusion), channel_id=1, replica_groups=mesh['ctx'=16,'fsdp'=32] {'ctx'}, dimensions={0}, use_global_device_ids=true | all-gather | bytes 557056 | tf_op jit(solution)/shard_map/all_gather | solution.py:105
  310.6 27.7 %all_gather.22 = bf16[128,2048]{1,0:T(8,128)(2,1)S(1)} all-gather(bf16[8,2048]{1,0:T(8,128)(2,1)S(1)} %convolution_convert_fusion.1), channel_id=1, replica_groups=mesh['ctx'=16,'fsdp'=32] {'ctx'}, dimensions={0}, use_global_device_ids=true | all-gather | bytes 557056 | tf_op jit(solution)/shard_map/all_gather | solution.py:106
  338.3 3.2 fusion.55
  341.5 2.5 convolution_multiply_fusion.3
  344.0 71.4 %all-gather.6.cloned.1.call-done = bf16[2048,448]{1,0:T(8,128)(2,1)} async-done(((bf16[64,448]{1,0:T(8,128)(2,1)}), bf16[2048,448]{1,0:T(8,128)(2,1)}) %all-gather.6.cloned.1.call-update) | async-done | bytes 1835024 | tf_op jit(solution)/shard_map/all_gather | solution.py:33
  415.4 5.5 %fusion.15 = f32[128,2048]{1,0:T(8,128)} fusion(bf16[2048,448]{1,0:T(8,128)(2,1)} %all-gather.8.cloned.1.call-done, f32[128,448]{0,1:T(8,128)S(1)} %convolution_multiply_fusion.3, bf16[128,2048]{1,0:T(8,128)(2,1)S(1)} %all_gather.25, bf16[2048,448]{1,0:T(8,128)(2,1)} %all-gather.6.cloned.1.call-done, f32[128,448]{0,1:T(8,128)} %fusion.55), kind=kOutput, calls=%fused_computation.27 | convolution fusion | flops 470335488 | bytes 5701632 | tf_op jit(solution)/shard_map/dot_general | solution.py:121
  420.8 3.5 fusion.9
  426.0 86.1 %reduce-scatter.2.cloned.1.call-done = bf16[8,2048]{1,0:T(8,128)(2,1)} async-done(((bf16[128,2048]{1,0:T(8,128)(2,1)}), bf16[8,2048]{1,0:T(8,128)(2,1)}) %reduce-scatter.2.cloned.1.call-update) | async-done | bytes 32784 | tf_op jit(solution)/shard_map/reduce_scatter | solution.py:124
  (243 shorter events, 111.7 us)
Async XLA Ops:
  7.2 331.1 %all-gather.8.cloned.1.call-start = ((), (), s32[]{:S(2)}) async-start(), calls=%async_computation.3 | async-start | bytes 2162688 | tf_op jit(solution)/shard_map/all_gather | solution.py:32
  7.9 333.6 %all-gather.4.cloned.1.call-start = ((), (), s32[]{:S(2)}) async-start(), calls=%async_computation.1 | async-start | bytes 2162688 | tf_op jit(solution)/shard_map/all_gather | solution.py:34
  8.7 406.7 %all-gather.6.cloned.1.call-start = ((), (), s32[]{:S(2)}) async-start(), calls=%async_computation.2 | async-start | bytes 2162688 | tf_op jit(solution)/shard_map/all_gather | solution.py:33
  9.4 502.6 %reduce-scatter.2.cloned.1.call-start = ((), (), s32[]{:S(2)}) async-start(), calls=%async_computation.4 | async-start | bytes 557056 | tf_op jit(solution)/shard_map/reduce_scatter | solution.py:124
  40.9 10.2 %collective-permute-start = (bf16[128,512]{0,1:T(8,128)(2,1)S(1)}, bf16[128,512]{0,1:T(8,128)(2,1)S(1)}, u32[]{:S(2)}, u32[]{:S(2)}) collective-permute-start(bf16[128,512]{0,1:T(8,128)(2,1)S(1)} %get-tuple-element.383), channel_id=1, source_target_pairs={{0,32},{32,64},{64,96},{96,128},{128,160},{160,192},{192,224},{224... | collective-permute-start | bytes 393224 | tf_op jit(solution)/shard_map/while/body/eval_jaxpr/ppermute | solution.py:16
  43.1 11.3 %collective-permute-start.1 = (bf16[128,512]{0,1:T(8,128)(2,1)S(1)}, bf16[128,512]{0,1:T(8,128)(2,1)S(1)}, u32[]{:S(2)}, u32[]{:S(2)}) collective-permute-start(bf16[128,512]{0,1:T(8,128)(2,1)S(1)} %get-tuple-element.384), channel_id=1, source_target_pairs={{0,32},{32,64},{64,96},{96,128},{128,160},{160,192},{192,224},{224... | collective-permute-start | bytes 393224 | tf_op jit(solution)/shard_map/while/body/eval_jaxpr/ppermute | solution.py:16
  55.2 11.1 %collective-permute-start = (bf16[128,512]{0,1:T(8,128)(2,1)S(1)}, bf16[128,512]{0,1:T(8,128)(2,1)S(1)}, u32[]{:S(2)}, u32[]{:S(2)}) collective-permute-start(bf16[128,512]{0,1:T(8,128)(2,1)S(1)} %get-tuple-element.383), channel_id=1, source_target_pairs={{0,32},{32,64},{64,96},{96,128},{128,160},{160,192},{192,224},{224... | collective-permute-start | bytes 393224 | tf_op jit(solution)/shard_map/while/body/eval_jaxpr/ppermute | solution.py:16
  57.1 11.6 %collective-permute-start.1 = (bf16[128,512]{0,1:T(8,128)(2,1)S(1)}, bf16[128,512]{0,1:T(8,128)(2,1)S(1)}, u32[]{:S(2)}, u32[]{:S(2)}) collective-permute-start(bf16[128,512]{0,1:T(8,128)(2,1)S(1)} %get-tuple-element.384), channel_id=1, source_target_pairs={{0,32},{32,64},{64,96},{96,128},{128,160},{160,192},{192,224},{224... | collective-permute-start | bytes 393224 | tf_op jit(solution)/shard_map/while/body/eval_jaxpr/ppermute | solution.py:16
  69.4 11.0 %collective-permute-start = (bf16[128,512]{0,1:T(8,128)(2,1)S(1)}, bf16[128,512]{0,1:T(8,128)(2,1)S(1)}, u32[]{:S(2)}, u32[]{:S(2)}) collective-permute-start(bf16[128,512]{0,1:T(8,128)(2,1)S(1)} %get-tuple-element.383), channel_id=1, source_target_pairs={{0,32},{32,64},{64,96},{96,128},{128,160},{160,192},{192,224},{224... | collective-permute-start | bytes 393224 | tf_op jit(solution)/shard_map/while/body/eval_jaxpr/ppermute | solution.py:16
  71.3 11.3 %collective-permute-start.1 = (bf16[128,512]{0,1:T(8,128)(2,1)S(1)}, bf16[128,512]{0,1:T(8,128)(2,1)S(1)}, u32[]{:S(2)}, u32[]{:S(2)}) collective-permute-start(bf16[128,512]{0,1:T(8,128)(2,1)S(1)} %get-tuple-element.384), channel_id=1, source_target_pairs={{0,32},{32,64},{64,96},{96,128},{128,160},{160,192},{192,224},{224... | collective-permute-start | bytes 393224 | tf_op jit(solution)/shard_map/while/body/eval_jaxpr/ppermute | solution.py:16
  83.4 11.4 %collective-permute-start = (bf16[128,512]{0,1:T(8,128)(2,1)S(1)}, bf16[128,512]{0,1:T(8,128)(2,1)S(1)}, u32[]{:S(2)}, u32[]{:S(2)}) collective-permute-start(bf16[128,512]{0,1:T(8,128)(2,1)S(1)} %get-tuple-element.383), channel_id=1, source_target_pairs={{0,32},{32,64},{64,96},{96,128},{128,160},{160,192},{192,224},{224... | collective-permute-start | bytes 393224 | tf_op jit(solution)/shard_map/while/body/eval_jaxpr/ppermute | solution.py:16
  85.3 11.3 %collective-permute-start.1 = (bf16[128,512]{0,1:T(8,128)(2,1)S(1)}, bf16[128,512]{0,1:T(8,128)(2,1)S(1)}, u32[]{:S(2)}, u32[]{:S(2)}) collective-permute-start(bf16[128,512]{0,1:T(8,128)(2,1)S(1)} %get-tuple-element.384), channel_id=1, source_target_pairs={{0,32},{32,64},{64,96},{96,128},{128,160},{160,192},{192,224},{224... | collective-permute-start | bytes 393224 | tf_op jit(solution)/shard_map/while/body/eval_jaxpr/ppermute | solution.py:16
  97.4 11.2 %collective-permute-start = (bf16[128,512]{0,1:T(8,128)(2,1)S(1)}, bf16[128,512]{0,1:T(8,128)(2,1)S(1)}, u32[]{:S(2)}, u32[]{:S(2)}) collective-permute-start(bf16[128,512]{0,1:T(8,128)(2,1)S(1)} %get-tuple-element.383), channel_id=1, source_target_pairs={{0,32},{32,64},{64,96},{96,128},{128,160},{160,192},{192,224},{224... | collective-permute-start | bytes 393224 | tf_op jit(solution)/shard_map/while/body/eval_jaxpr/ppermute | solution.py:16
  99.3 11.7 %collective-permute-start.1 = (bf16[128,512]{0,1:T(8,128)(2,1)S(1)}, bf16[128,512]{0,1:T(8,128)(2,1)S(1)}, u32[]{:S(2)}, u32[]{:S(2)}) collective-permute-start(bf16[128,512]{0,1:T(8,128)(2,1)S(1)} %get-tuple-element.384), channel_id=1, source_target_pairs={{0,32},{32,64},{64,96},{96,128},{128,160},{160,192},{192,224},{224... | collective-permute-start | bytes 393224 | tf_op jit(solution)/shard_map/while/body/eval_jaxpr/ppermute | solution.py:16
  111.7 10.4 %collective-permute-start = (bf16[128,512]{0,1:T(8,128)(2,1)S(1)}, bf16[128,512]{0,1:T(8,128)(2,1)S(1)}, u32[]{:S(2)}, u32[]{:S(2)}) collective-permute-start(bf16[128,512]{0,1:T(8,128)(2,1)S(1)} %get-tuple-element.383), channel_id=1, source_target_pairs={{0,32},{32,64},{64,96},{96,128},{128,160},{160,192},{192,224},{224... | collective-permute-start | bytes 393224 | tf_op jit(solution)/shard_map/while/body/eval_jaxpr/ppermute | solution.py:16
  113.7 11.2 %collective-permute-start.1 = (bf16[128,512]{0,1:T(8,128)(2,1)S(1)}, bf16[128,512]{0,1:T(8,128)(2,1)S(1)}, u32[]{:S(2)}, u32[]{:S(2)}) collective-permute-start(bf16[128,512]{0,1:T(8,128)(2,1)S(1)} %get-tuple-element.384), channel_id=1, source_target_pairs={{0,32},{32,64},{64,96},{96,128},{128,160},{160,192},{192,224},{224... | collective-permute-start | bytes 393224 | tf_op jit(solution)/shard_map/while/body/eval_jaxpr/ppermute | solution.py:16
  125.6 10.4 %collective-permute-start = (bf16[128,512]{0,1:T(8,128)(2,1)S(1)}, bf16[128,512]{0,1:T(8,128)(2,1)S(1)}, u32[]{:S(2)}, u32[]{:S(2)}) collective-permute-start(bf16[128,512]{0,1:T(8,128)(2,1)S(1)} %get-tuple-element.383), channel_id=1, source_target_pairs={{0,32},{32,64},{64,96},{96,128},{128,160},{160,192},{192,224},{224... | collective-permute-start | bytes 393224 | tf_op jit(solution)/shard_map/while/body/eval_jaxpr/ppermute | solution.py:16
  127.5 10.2 %collective-permute-start.1 = (bf16[128,512]{0,1:T(8,128)(2,1)S(1)}, bf16[128,512]{0,1:T(8,128)(2,1)S(1)}, u32[]{:S(2)}, u32[]{:S(2)}) collective-permute-start(bf16[128,512]{0,1:T(8,128)(2,1)S(1)} %get-tuple-element.384), channel_id=1, source_target_pairs={{0,32},{32,64},{64,96},{96,128},{128,160},{160,192},{192,224},{224... | collective-permute-start | bytes 393224 | tf_op jit(solution)/shard_map/while/body/eval_jaxpr/ppermute | solution.py:16
  138.4 10.3 %collective-permute-start = (bf16[128,512]{0,1:T(8,128)(2,1)S(1)}, bf16[128,512]{0,1:T(8,128)(2,1)S(1)}, u32[]{:S(2)}, u32[]{:S(2)}) collective-permute-start(bf16[128,512]{0,1:T(8,128)(2,1)S(1)} %get-tuple-element.383), channel_id=1, source_target_pairs={{0,32},{32,64},{64,96},{96,128},{128,160},{160,192},{192,224},{224... | collective-permute-start | bytes 393224 | tf_op jit(solution)/shard_map/while/body/eval_jaxpr/ppermute | solution.py:16
  140.4 10.0 %collective-permute-start.1 = (bf16[128,512]{0,1:T(8,128)(2,1)S(1)}, bf16[128,512]{0,1:T(8,128)(2,1)S(1)}, u32[]{:S(2)}, u32[]{:S(2)}) collective-permute-start(bf16[128,512]{0,1:T(8,128)(2,1)S(1)} %get-tuple-element.384), channel_id=1, source_target_pairs={{0,32},{32,64},{64,96},{96,128},{128,160},{160,192},{192,224},{224... | collective-permute-start | bytes 393224 | tf_op jit(solution)/shard_map/while/body/eval_jaxpr/ppermute | solution.py:16
  163.6 10.3 %collective-permute-start = (bf16[128,512]{0,1:T(8,128)(2,1)S(1)}, bf16[128,512]{0,1:T(8,128)(2,1)S(1)}, u32[]{:S(2)}, u32[]{:S(2)}) collective-permute-start(bf16[128,512]{0,1:T(8,128)(2,1)S(1)} %get-tuple-element.383), channel_id=1, source_target_pairs={{0,32},{32,64},{64,96},{96,128},{128,160},{160,192},{192,224},{224... | collective-permute-start | bytes 393224 | tf_op jit(solution)/shard_map/while/body/eval_jaxpr/ppermute | solution.py:16
  165.6 11.3 %collective-permute-start.1 = (bf16[128,512]{0,1:T(8,128)(2,1)S(1)}, bf16[128,512]{0,1:T(8,128)(2,1)S(1)}, u32[]{:S(2)}, u32[]{:S(2)}) collective-permute-start(bf16[128,512]{0,1:T(8,128)(2,1)S(1)} %get-tuple-element.384), channel_id=1, source_target_pairs={{0,32},{32,64},{64,96},{96,128},{128,160},{160,192},{192,224},{224... | collective-permute-start | bytes 393224 | tf_op jit(solution)/shard_map/while/body/eval_jaxpr/ppermute | solution.py:16
  177.6 11.0 %collective-permute-start = (bf16[128,512]{0,1:T(8,128)(2,1)S(1)}, bf16[128,512]{0,1:T(8,128)(2,1)S(1)}, u32[]{:S(2)}, u32[]{:S(2)}) collective-permute-start(bf16[128,512]{0,1:T(8,128)(2,1)S(1)} %get-tuple-element.383), channel_id=1, source_target_pairs={{0,32},{32,64},{64,96},{96,128},{128,160},{160,192},{192,224},{224... | collective-permute-start | bytes 393224 | tf_op jit(solution)/shard_map/while/body/eval_jaxpr/ppermute | solution.py:16
  179.5 11.4 %collective-permute-start.1 = (bf16[128,512]{0,1:T(8,128)(2,1)S(1)}, bf16[128,512]{0,1:T(8,128)(2,1)S(1)}, u32[]{:S(2)}, u32[]{:S(2)}) collective-permute-start(bf16[128,512]{0,1:T(8,128)(2,1)S(1)} %get-tuple-element.384), channel_id=1, source_target_pairs={{0,32},{32,64},{64,96},{96,128},{128,160},{160,192},{192,224},{224... | collective-permute-start | bytes 393224 | tf_op jit(solution)/shard_map/while/body/eval_jaxpr/ppermute | solution.py:16
  191.6 11.1 %collective-permute-start = (bf16[128,512]{0,1:T(8,128)(2,1)S(1)}, bf16[128,512]{0,1:T(8,128)(2,1)S(1)}, u32[]{:S(2)}, u32[]{:S(2)}) collective-permute-start(bf16[128,512]{0,1:T(8,128)(2,1)S(1)} %get-tuple-element.383), channel_id=1, source_target_pairs={{0,32},{32,64},{64,96},{96,128},{128,160},{160,192},{192,224},{224... | collective-permute-start | bytes 393224 | tf_op jit(solution)/shard_map/while/body/eval_jaxpr/ppermute | solution.py:16
  193.5 11.6 %collective-permute-start.1 = (bf16[128,512]{0,1:T(8,128)(2,1)S(1)}, bf16[128,512]{0,1:T(8,128)(2,1)S(1)}, u32[]{:S(2)}, u32[]{:S(2)}) collective-permute-start(bf16[128,512]{0,1:T(8,128)(2,1)S(1)} %get-tuple-element.384), channel_id=1, source_target_pairs={{0,32},{32,64},{64,96},{96,128},{128,160},{160,192},{192,224},{224... | collective-permute-start | bytes 393224 | tf_op jit(solution)/shard_map/while/body/eval_jaxpr/ppermute | solution.py:16
  205.8 10.9 %collective-permute-start = (bf16[128,512]{0,1:T(8,128)(2,1)S(1)}, bf16[128,512]{0,1:T(8,128)(2,1)S(1)}, u32[]{:S(2)}, u32[]{:S(2)}) collective-permute-start(bf16[128,512]{0,1:T(8,128)(2,1)S(1)} %get-tuple-element.383), channel_id=1, source_target_pairs={{0,32},{32,64},{64,96},{96,128},{128,160},{160,192},{192,224},{224... | collective-permute-start | bytes 393224 | tf_op jit(solution)/shard_map/while/body/eval_jaxpr/ppermute | solution.py:16
  207.7 11.4 %collective-permute-start.1 = (bf16[128,512]{0,1:T(8,128)(2,1)S(1)}, bf16[128,512]{0,1:T(8,128)(2,1)S(1)}, u32[]{:S(2)}, u32[]{:S(2)}) collective-permute-start(bf16[128,512]{0,1:T(8,128)(2,1)S(1)} %get-tuple-element.384), channel_id=1, source_target_pairs={{0,32},{32,64},{64,96},{96,128},{128,160},{160,192},{192,224},{224... | collective-permute-start | bytes 393224 | tf_op jit(solution)/shard_map/while/body/eval_jaxpr/ppermute | solution.py:16
  219.9 10.3 %collective-permute-start = (bf16[128,512]{0,1:T(8,128)(2,1)S(1)}, bf16[128,512]{0,1:T(8,128)(2,1)S(1)}, u32[]{:S(2)}, u32[]{:S(2)}) collective-permute-start(bf16[128,512]{0,1:T(8,128)(2,1)S(1)} %get-tuple-element.383), channel_id=1, source_target_pairs={{0,32},{32,64},{64,96},{96,128},{128,160},{160,192},{192,224},{224... | collective-permute-start | bytes 393224 | tf_op jit(solution)/shard_map/while/body/eval_jaxpr/ppermute | solution.py:16
  221.8 11.1 %collective-permute-start.1 = (bf16[128,512]{0,1:T(8,128)(2,1)S(1)}, bf16[128,512]{0,1:T(8,128)(2,1)S(1)}, u32[]{:S(2)}, u32[]{:S(2)}) collective-permute-start(bf16[128,512]{0,1:T(8,128)(2,1)S(1)} %get-tuple-element.384), channel_id=1, source_target_pairs={{0,32},{32,64},{64,96},{96,128},{128,160},{160,192},{192,224},{224... | collective-permute-start | bytes 393224 | tf_op jit(solution)/shard_map/while/body/eval_jaxpr/ppermute | solution.py:16
  233.6 10.3 %collective-permute-start = (bf16[128,512]{0,1:T(8,128)(2,1)S(1)}, bf16[128,512]{0,1:T(8,128)(2,1)S(1)}, u32[]{:S(2)}, u32[]{:S(2)}) collective-permute-start(bf16[128,512]{0,1:T(8,128)(2,1)S(1)} %get-tuple-element.383), channel_id=1, source_target_pairs={{0,32},{32,64},{64,96},{96,128},{128,160},{160,192},{192,224},{224... | collective-permute-start | bytes 393224 | tf_op jit(solution)/shard_map/while/body/eval_jaxpr/ppermute | solution.py:16
  235.6 11.3 %collective-permute-start.1 = (bf16[128,512]{0,1:T(8,128)(2,1)S(1)}, bf16[128,512]{0,1:T(8,128)(2,1)S(1)}, u32[]{:S(2)}, u32[]{:S(2)}) collective-permute-start(bf16[128,512]{0,1:T(8,128)(2,1)S(1)} %get-tuple-element.384), channel_id=1, source_target_pairs={{0,32},{32,64},{64,96},{96,128},{128,160},{160,192},{192,224},{224... | collective-permute-start | bytes 393224 | tf_op jit(solution)/shard_map/while/body/eval_jaxpr/ppermute | solution.py:16
  (6 other events, 385.9 us)
Sparse Core Ops, SparseCore 0:
  10.1 136.2 all-gather.7
  148.5 132.0 all-gather.3
  282.6 132.7 all-gather.5
  424.5 87.4 reduce-scatter.1
where the time goes:
time: 522 us; the launch traced here: 521 us
  waiting for transfers between devices  285 us (55%)
  blocking collectives  108 us (21%)
  starting transfers between devices  58.1 us (11%)
  matrix products  32.9 us (6%)
  between operations  14.6 us (3%)
  local copies, waits for them, and re-layouts  13.6 us (3%)
  other arithmetic  6.84 us (1%)
    ppermute x30, waiting for transfers between devices, from_behind(): lax.ppermute(shard, axis, [(i, (i + by) % length) for i in range(length)])  125 us
    reduce_scatter x1, waiting for transfers between devices, on_device(): lax.psum_scatter((result + lax.dot_general(grad_up, up_panel, contract_la...  86.1 us
    all_gather x1, waiting for transfers between devices, on_device(): lax.all_gather(up_weight, 'fsdp', axis=0, tiled=True)  71.4 us
    ppermute x30, starting transfers between devices, from_behind(): lax.ppermute(shard, axis, [(i, (i + by) % length) for i in range(length)])  57.9 us
    unnamed x1, blocking collectives  33.2 us
    all_gather x1, blocking collectives, on_device(): lax.all_gather(slot_dy, 'ctx', axis=0, tiled=True)  27.7 us
    all_gather x1, blocking collectives, on_device(): every_doc = lax.all_gather(doc_ids, 'ctx', axis=1, tiled=True)[0]  24.6 us
    all_gather x1, blocking collectives, on_device(): lax.all_gather(slot_x, 'ctx', axis=0, tiled=True)  22.7 us
  transfers between devices with their start and end apart: 34, of which 32 were waited for; matrix products, arithmetic and copies ran while one was open for 8% of the time, Pallas kernels for 0%

commit v1 on v0

--- a/solution.py
+++ b/solution.py
@@ -30,7 +30,9 @@
 ):
     gate_panel, up_panel, down_panel = (
         lax.all_gather(gate_weight, "fsdp", axis=0, tiled=True),
-        lax.all_gather(up_weight, "fsdp", axis=0, tiled=True),
+        jnp.concatenate(
+            lax.all_to_all(jnp.stack([up_weight] * lax.axis_size("fsdp")), "fsdp", 0, 0), axis=0
+        ),
         lax.all_gather(down_weight, "fsdp", axis=1, tiled=True),
     )
     every_doc = lax.all_gather(doc_ids, "ctx", axis=1, tiled=True)[0]

time: 522 us -> 461 us (0.88)
  waiting for transfers between devices: 285 us -> 214 us
  starting transfers between devices: 58.1 us -> 74.5 us
    all_gather x1 -> x0, waiting for transfers between devices: 71.4 us -> none  [on_device(): lax.all_gather(up_weight, 'fsdp', axis=0, tiled=True)]
    all_to_all x0 -> x1, starting transfers between devices: none -> 16.5 us  [on_device(): lax.all_to_all(jnp.stack([up_weight] * lax.axis_size('fsdp')), 'fsdp', 0, 0)]
    all_gather x1, blocking collectives: 27.7 us -> 21.6 us  [on_device(): lax.all_gather(slot_dy, 'ctx', axis=0, tiled=True)]
  transfers between devices with their start and end apart: 34 -> 34, of which waited for: 32 -> 31; matrix products, arithmetic and copies ran while one was open for 8% -> 9% of each run, Pallas kernels for 0% -> 0%
where the time goes in v1:
time: 461 us; the launch traced here: 460 us
  waiting for transfers between devices  214 us (46%)
  blocking collectives  104 us (23%)
  starting transfers between devices  74.5 us (16%)
  matrix products  32.9 us (7%)
  between operations  14.6 us (3%)
  local copies, waits for them, and re-layouts  11.4 us (2%)
  other arithmetic  6.84 us (1%)
    ppermute x30, waiting for transfers between devices, from_behind(): lax.ppermute(shard, axis, [(i, (i + by) % length) for i in range(length)])  130 us
    reduce_scatter x1, waiting for transfers between devices, on_device(): lax.psum_scatter((result + lax.dot_general(grad_up, up_panel, contract_la...  82.6 us
    ppermute x30, starting transfers between devices, from_behind(): lax.ppermute(shard, axis, [(i, (i + by) % length) for i in range(length)])  57.9 us
    unnamed x1, blocking collectives  33.4 us
    all_gather x1, blocking collectives, on_device(): lax.all_gather(slot_x, 'ctx', axis=0, tiled=True)  24.4 us
    all_gather x1, blocking collectives, on_device(): every_doc = lax.all_gather(doc_ids, 'ctx', axis=1, tiled=True)[0]  24.1 us
    all_gather x1, blocking collectives, on_device(): lax.all_gather(slot_dy, 'ctx', axis=0, tiled=True)  21.6 us
    all_to_all x1, starting transfers between devices, on_device(): lax.all_to_all(jnp.stack([up_weight] * lax.axis_size('fsdp')), 'fsdp', 0, 0)  16.5 us
  transfers between devices with their start and end apart: 34, of which 31 were waited for; matrix products, arithmetic and copies ran while one was open for 9% of the time, Pallas kernels for 0%

profile of v1, /device:TPU:32, one launch (start us, length us, event | category | flops | bytes accessed | tf_op | source)
XLA Modules:
  0.0 460.0 jit_solution(8201696028737586967)
XLA Ops:
  7.9 2.4 stack.2
  10.3 16.5 %all-to-all-start = ((bf16[32,64,448]{2,1,0:T(8,128)(2,1)}), bf16[32,64,448]{2,1,0:T(8,128)(2,1)}, u32[]{:S(2)}, u32[]{:S(2)}) async-start(bf16[32,64,448]{2,1,0:T(8,128)(2,1)} %stack.2), calls=%async_computation | async-start | bytes 4194304 | tf_op jit(solution)/shard_map/all_to_all | solution.py:34
  28.3 24.1 %all_gather.18 = s32[1,2048]{1,0:T(1,128)S(1)} all-gather(s32[1,128]{1,0:T(1,128)S(1)} %copy-done.6), channel_id=1, replica_groups=mesh['ctx'=16,'fsdp'=32] {'ctx'}, dimensions={1}, use_global_device_ids=true | all-gather | bytes 8704 | tf_op jit(solution)/shard_map/all_gather | solution.py:38
  53.9 211.8 %while.23 = (s32[]{:T(128)}, f32[4,4,128]{2,1,0:T(4,128)S(1)}, f32[4,4,128]{2,1,0:T(4,128)S(1)}, f32[4,4,128,128]{3,2,1,0:T(8,128)S(1)}, bf16[128,512]{0,1:T(8,1...) while((s32[]{:T(128)}, f32[4,4,128]{2,1,0:T(4,128)S(1)}, ...), condition=%wide.region_5.6_spmd, body=%wide.region_2.5_spmd.sunk | while | flops 137121808 | bytes 7801232 | solution.py:84
  53.9 2.3 collective-permute-start
  58.3 8.2 %collective-permute-done = bf16[128,512]{0,1:T(8,128)(2,1)S(1)} collective-permute-done((bf16[128,512]{0,1:T(8,128)(2,1)S(1)}, bf16[128,512]{0,1:T(8,128)(2,1)S(1)}, u32[]{:S(2)}, u32[]{:S(2)}) %collective-permute-start) | collective-permute-done | bytes 131104 | tf_op jit(solution)/shard_map/while/body/eval_jaxpr/ppermute | solution.py:16
  73.2 8.1 %collective-permute-done = bf16[128,512]{0,1:T(8,128)(2,1)S(1)} collective-permute-done((bf16[128,512]{0,1:T(8,128)(2,1)S(1)}, bf16[128,512]{0,1:T(8,128)(2,1)S(1)}, u32[]{:S(2)}, u32[]{:S(2)}) %collective-permute-start) | collective-permute-done | bytes 131104 | tf_op jit(solution)/shard_map/while/body/eval_jaxpr/ppermute | solution.py:16
  81.9 2.2 collective-permute-done.1
  88.9 7.2 %collective-permute-done = bf16[128,512]{0,1:T(8,128)(2,1)S(1)} collective-permute-done((bf16[128,512]{0,1:T(8,128)(2,1)S(1)}, bf16[128,512]{0,1:T(8,128)(2,1)S(1)}, u32[]{:S(2)}, u32[]{:S(2)}) %collective-permute-start) | collective-permute-done | bytes 131104 | tf_op jit(solution)/shard_map/while/body/eval_jaxpr/ppermute | solution.py:16
  96.7 3.2 collective-permute-done.1
  104.7 6.9 %collective-permute-done = bf16[128,512]{0,1:T(8,128)(2,1)S(1)} collective-permute-done((bf16[128,512]{0,1:T(8,128)(2,1)S(1)}, bf16[128,512]{0,1:T(8,128)(2,1)S(1)}, u32[]{:S(2)}, u32[]{:S(2)}) %collective-permute-start) | collective-permute-done | bytes 131104 | tf_op jit(solution)/shard_map/while/body/eval_jaxpr/ppermute | solution.py:16
  112.2 2.5 collective-permute-done.1
  119.4 6.3 %collective-permute-done = bf16[128,512]{0,1:T(8,128)(2,1)S(1)} collective-permute-done((bf16[128,512]{0,1:T(8,128)(2,1)S(1)}, bf16[128,512]{0,1:T(8,128)(2,1)S(1)}, u32[]{:S(2)}, u32[]{:S(2)}) %collective-permute-start) | collective-permute-done | bytes 131104 | tf_op jit(solution)/shard_map/while/body/eval_jaxpr/ppermute | solution.py:16
  133.1 6.6 %collective-permute-done = bf16[128,512]{0,1:T(8,128)(2,1)S(1)} collective-permute-done((bf16[128,512]{0,1:T(8,128)(2,1)S(1)}, bf16[128,512]{0,1:T(8,128)(2,1)S(1)}, u32[]{:S(2)}, u32[]{:S(2)}) %collective-permute-start) | collective-permute-done | bytes 131104 | tf_op jit(solution)/shard_map/while/body/eval_jaxpr/ppermute | solution.py:16
  146.7 6.8 %collective-permute-done = bf16[128,512]{0,1:T(8,128)(2,1)S(1)} collective-permute-done((bf16[128,512]{0,1:T(8,128)(2,1)S(1)}, bf16[128,512]{0,1:T(8,128)(2,1)S(1)}, u32[]{:S(2)}, u32[]{:S(2)}) %collective-permute-start) | collective-permute-done | bytes 131104 | tf_op jit(solution)/shard_map/while/body/eval_jaxpr/ppermute | solution.py:16
  160.8 6.3 %collective-permute-done = bf16[128,512]{0,1:T(8,128)(2,1)S(1)} collective-permute-done((bf16[128,512]{0,1:T(8,128)(2,1)S(1)}, bf16[128,512]{0,1:T(8,128)(2,1)S(1)}, u32[]{:S(2)}, u32[]{:S(2)}) %collective-permute-start) | collective-permute-done | bytes 131104 | tf_op jit(solution)/shard_map/while/body/eval_jaxpr/ppermute | solution.py:16
  173.8 5.9 %collective-permute-done = bf16[128,512]{0,1:T(8,128)(2,1)S(1)} collective-permute-done((bf16[128,512]{0,1:T(8,128)(2,1)S(1)}, bf16[128,512]{0,1:T(8,128)(2,1)S(1)}, u32[]{:S(2)}, u32[]{:S(2)}) %collective-permute-start) | collective-permute-done | bytes 131104 | tf_op jit(solution)/shard_map/while/body/eval_jaxpr/ppermute | solution.py:16
  186.4 5.8 %collective-permute-done = bf16[128,512]{0,1:T(8,128)(2,1)S(1)} collective-permute-done((bf16[128,512]{0,1:T(8,128)(2,1)S(1)}, bf16[128,512]{0,1:T(8,128)(2,1)S(1)}, u32[]{:S(2)}, u32[]{:S(2)}) %collective-permute-start) | collective-permute-done | bytes 131104 | tf_op jit(solution)/shard_map/while/body/eval_jaxpr/ppermute | solution.py:16
  198.9 7.3 %collective-permute-done = bf16[128,512]{0,1:T(8,128)(2,1)S(1)} collective-permute-done((bf16[128,512]{0,1:T(8,128)(2,1)S(1)}, bf16[128,512]{0,1:T(8,128)(2,1)S(1)}, u32[]{:S(2)}, u32[]{:S(2)}) %collective-permute-start) | collective-permute-done | bytes 131104 | tf_op jit(solution)/shard_map/while/body/eval_jaxpr/ppermute | solution.py:16
  213.3 5.9 %collective-permute-done = bf16[128,512]{0,1:T(8,128)(2,1)S(1)} collective-permute-done((bf16[128,512]{0,1:T(8,128)(2,1)S(1)}, bf16[128,512]{0,1:T(8,128)(2,1)S(1)}, u32[]{:S(2)}, u32[]{:S(2)}) %collective-permute-start) | collective-permute-done | bytes 131104 | tf_op jit(solution)/shard_map/while/body/eval_jaxpr/ppermute | solution.py:16
  219.9 2.5 collective-permute-done.1
  227.2 6.8 %collective-permute-done = bf16[128,512]{0,1:T(8,128)(2,1)S(1)} collective-permute-done((bf16[128,512]{0,1:T(8,128)(2,1)S(1)}, bf16[128,512]{0,1:T(8,128)(2,1)S(1)}, u32[]{:S(2)}, u32[]{:S(2)}) %collective-permute-start) | collective-permute-done | bytes 131104 | tf_op jit(solution)/shard_map/while/body/eval_jaxpr/ppermute | solution.py:16
  240.9 7.0 %collective-permute-done = bf16[128,512]{0,1:T(8,128)(2,1)S(1)} collective-permute-done((bf16[128,512]{0,1:T(8,128)(2,1)S(1)}, bf16[128,512]{0,1:T(8,128)(2,1)S(1)}, u32[]{:S(2)}, u32[]{:S(2)}) %collective-permute-start) | collective-permute-done | bytes 131104 | tf_op jit(solution)/shard_map/while/body/eval_jaxpr/ppermute | solution.py:16
  255.5 6.8 %collective-permute-done = bf16[128,512]{0,1:T(8,128)(2,1)S(1)} collective-permute-done((bf16[128,512]{0,1:T(8,128)(2,1)S(1)}, bf16[128,512]{0,1:T(8,128)(2,1)S(1)}, u32[]{:S(2)}, u32[]{:S(2)}) %collective-permute-start) | collective-permute-done | bytes 131104 | tf_op jit(solution)/shard_map/while/body/eval_jaxpr/ppermute | solution.py:16
  272.4 33.4 %all-reduce = bf16[128]{0:T(256)(128)(2,1)S(1)} all-reduce(bf16[128]{0:T(256)(128)(2,1)S(1)} %dynamic-update-slice), channel_id=1, replica_groups=mesh['ctx'=16,'fsdp'=32] {'ctx'}, use_global_device_ids=true, to_apply=%add | all-reduce | flops 128 | bytes 512
  306.0 21.6 %all_gather.19 = bf16[128,2048]{1,0:T(8,128)(2,1)S(1)} all-gather(bf16[8,2048]{1,0:T(8,128)(2,1)S(1)} %convolution_convert_fusion.1), channel_id=1, replica_groups=mesh['ctx'=16,'fsdp'=32] {'ctx'}, dimensions={0}, use_global_device_ids=true | all-gather | bytes 557056 | tf_op jit(solution)/shard_map/all_gather | solution.py:108
  327.8 24.4 %all_gather.22 = bf16[128,2048]{1,0:T(8,128)(2,1)S(1)} all-gather(bf16[8,2048]{1,0:T(8,128)(2,1)S(1)} %convolution_convert_fusion), channel_id=1, replica_groups=mesh['ctx'=16,'fsdp'=32] {'ctx'}, dimensions={0}, use_global_device_ids=true | all-gather | bytes 557056 | tf_op jit(solution)/shard_map/all_gather | solution.py:107
  352.2 3.2 fusion.55
  355.4 2.5 convolution_multiply_fusion.3
  357.9 5.5 %fusion.15 = f32[128,2048]{1,0:T(8,128)} fusion(bf16[2048,448]{1,0:T(8,128)(2,1)} %all-gather.5.cloned.1.call-done, f32[128,448]{0,1:T(8,128)S(1)} %convolution_multiply_fusion.3, bf16[128,2048]{1,0:T(8,128)(2,1)S(1)} %all_gather.22, bf16[2048,448]{1,0:T(8,128)(2,1)} %bitcast.19, f32[128,448]{0,1:T(8,128)} %fusion.55), kind=kOutput, calls=%fused_computation.27 | convolution fusion | flops 470335488 | bytes 5701632 | tf_op jit(solution)/shard_map/dot_general | solution.py:123
  363.4 3.5 fusion.9
  368.6 82.6 %reduce-scatter.2.cloned.1.call-done = bf16[8,2048]{1,0:T(8,128)(2,1)} async-done(((bf16[128,2048]{1,0:T(8,128)(2,1)}), bf16[8,2048]{1,0:T(8,128)(2,1)}) %reduce-scatter.2.cloned.1.call-update) | async-done | bytes 32784 | tf_op jit(solution)/shard_map/reduce_scatter | solution.py:126
  (251 shorter events, 109.3 us)
Async XLA Ops:
  7.2 345.1 %all-gather.5.cloned.1.call-start = ((), (), s32[]{:S(2)}) async-start(), calls=%async_computation.3 | async-start | bytes 2162688 | tf_op jit(solution)/shard_map/all_gather | solution.py:32
  10.3 347.6 %all-to-all-start = ((bf16[32,64,448]{2,1,0:T(8,128)(2,1)}), bf16[32,64,448]{2,1,0:T(8,128)(2,1)}, u32[]{:S(2)}, u32[]{:S(2)}) async-start(bf16[32,64,448]{2,1,0:T(8,128)(2,1)} %stack.2), calls=%async_computation | async-start | bytes 4194304 | tf_op jit(solution)/shard_map/all_to_all | solution.py:34
  26.8 328.6 %all-gather.3.cloned.1.call-start = ((), (), s32[]{:S(2)}) async-start(), calls=%async_computation.2 | async-start | bytes 2162688 | tf_op jit(solution)/shard_map/all_gather | solution.py:36
  27.6 423.6 %reduce-scatter.2.cloned.1.call-start = ((), (), s32[]{:S(2)}) async-start(), calls=%async_computation.4 | async-start | bytes 557056 | tf_op jit(solution)/shard_map/reduce_scatter | solution.py:126
  53.9 12.6 %collective-permute-start = (bf16[128,512]{0,1:T(8,128)(2,1)S(1)}, bf16[128,512]{0,1:T(8,128)(2,1)S(1)}, u32[]{:S(2)}, u32[]{:S(2)}) collective-permute-start(bf16[128,512]{0,1:T(8,128)(2,1)S(1)} %get-tuple-element.383), channel_id=1, source_target_pairs={{0,32},{32,64},{64,96},{96,128},{128,160},{160,192},{192,224},{224... | collective-permute-start | bytes 393224 | tf_op jit(solution)/shard_map/while/body/eval_jaxpr/ppermute | solution.py:16
  56.2 12.2 %collective-permute-start.1 = (bf16[128,512]{0,1:T(8,128)(2,1)S(1)}, bf16[128,512]{0,1:T(8,128)(2,1)S(1)}, u32[]{:S(2)}, u32[]{:S(2)}) collective-permute-start(bf16[128,512]{0,1:T(8,128)(2,1)S(1)} %get-tuple-element.384), channel_id=1, source_target_pairs={{0,32},{32,64},{64,96},{96,128},{128,160},{160,192},{192,224},{224... | collective-permute-start | bytes 393224 | tf_op jit(solution)/shard_map/while/body/eval_jaxpr/ppermute | solution.py:16
  69.1 12.1 %collective-permute-start = (bf16[128,512]{0,1:T(8,128)(2,1)S(1)}, bf16[128,512]{0,1:T(8,128)(2,1)S(1)}, u32[]{:S(2)}, u32[]{:S(2)}) collective-permute-start(bf16[128,512]{0,1:T(8,128)(2,1)S(1)} %get-tuple-element.383), channel_id=1, source_target_pairs={{0,32},{32,64},{64,96},{96,128},{128,160},{160,192},{192,224},{224... | collective-permute-start | bytes 393224 | tf_op jit(solution)/shard_map/while/body/eval_jaxpr/ppermute | solution.py:16
  71.1 13.1 %collective-permute-start.1 = (bf16[128,512]{0,1:T(8,128)(2,1)S(1)}, bf16[128,512]{0,1:T(8,128)(2,1)S(1)}, u32[]{:S(2)}, u32[]{:S(2)}) collective-permute-start(bf16[128,512]{0,1:T(8,128)(2,1)S(1)} %get-tuple-element.384), channel_id=1, source_target_pairs={{0,32},{32,64},{64,96},{96,128},{128,160},{160,192},{192,224},{224... | collective-permute-start | bytes 393224 | tf_op jit(solution)/shard_map/while/body/eval_jaxpr/ppermute | solution.py:16
  84.9 11.2 %collective-permute-start = (bf16[128,512]{0,1:T(8,128)(2,1)S(1)}, bf16[128,512]{0,1:T(8,128)(2,1)S(1)}, u32[]{:S(2)}, u32[]{:S(2)}) collective-permute-start(bf16[128,512]{0,1:T(8,128)(2,1)S(1)} %get-tuple-element.383), channel_id=1, source_target_pairs={{0,32},{32,64},{64,96},{96,128},{128,160},{160,192},{192,224},{224... | collective-permute-start | bytes 393224 | tf_op jit(solution)/shard_map/while/body/eval_jaxpr/ppermute | solution.py:16
  86.8 13.1 %collective-permute-start.1 = (bf16[128,512]{0,1:T(8,128)(2,1)S(1)}, bf16[128,512]{0,1:T(8,128)(2,1)S(1)}, u32[]{:S(2)}, u32[]{:S(2)}) collective-permute-start(bf16[128,512]{0,1:T(8,128)(2,1)S(1)} %get-tuple-element.384), channel_id=1, source_target_pairs={{0,32},{32,64},{64,96},{96,128},{128,160},{160,192},{192,224},{224... | collective-permute-start | bytes 393224 | tf_op jit(solution)/shard_map/while/body/eval_jaxpr/ppermute | solution.py:16
  100.6 11.0 %collective-permute-start = (bf16[128,512]{0,1:T(8,128)(2,1)S(1)}, bf16[128,512]{0,1:T(8,128)(2,1)S(1)}, u32[]{:S(2)}, u32[]{:S(2)}) collective-permute-start(bf16[128,512]{0,1:T(8,128)(2,1)S(1)} %get-tuple-element.383), channel_id=1, source_target_pairs={{0,32},{32,64},{64,96},{96,128},{128,160},{160,192},{192,224},{224... | collective-permute-start | bytes 393224 | tf_op jit(solution)/shard_map/while/body/eval_jaxpr/ppermute | solution.py:16
  102.5 12.1 %collective-permute-start.1 = (bf16[128,512]{0,1:T(8,128)(2,1)S(1)}, bf16[128,512]{0,1:T(8,128)(2,1)S(1)}, u32[]{:S(2)}, u32[]{:S(2)}) collective-permute-start(bf16[128,512]{0,1:T(8,128)(2,1)S(1)} %get-tuple-element.384), channel_id=1, source_target_pairs={{0,32},{32,64},{64,96},{96,128},{128,160},{160,192},{192,224},{224... | collective-permute-start | bytes 393224 | tf_op jit(solution)/shard_map/while/body/eval_jaxpr/ppermute | solution.py:16
  115.4 10.4 %collective-permute-start = (bf16[128,512]{0,1:T(8,128)(2,1)S(1)}, bf16[128,512]{0,1:T(8,128)(2,1)S(1)}, u32[]{:S(2)}, u32[]{:S(2)}) collective-permute-start(bf16[128,512]{0,1:T(8,128)(2,1)S(1)} %get-tuple-element.383), channel_id=1, source_target_pairs={{0,32},{32,64},{64,96},{96,128},{128,160},{160,192},{192,224},{224... | collective-permute-start | bytes 393224 | tf_op jit(solution)/shard_map/while/body/eval_jaxpr/ppermute | solution.py:16
  117.3 11.0 %collective-permute-start.1 = (bf16[128,512]{0,1:T(8,128)(2,1)S(1)}, bf16[128,512]{0,1:T(8,128)(2,1)S(1)}, u32[]{:S(2)}, u32[]{:S(2)}) collective-permute-start(bf16[128,512]{0,1:T(8,128)(2,1)S(1)} %get-tuple-element.384), channel_id=1, source_target_pairs={{0,32},{32,64},{64,96},{96,128},{128,160},{160,192},{192,224},{224... | collective-permute-start | bytes 393224 | tf_op jit(solution)/shard_map/while/body/eval_jaxpr/ppermute | solution.py:16
  129.1 10.7 %collective-permute-start = (bf16[128,512]{0,1:T(8,128)(2,1)S(1)}, bf16[128,512]{0,1:T(8,128)(2,1)S(1)}, u32[]{:S(2)}, u32[]{:S(2)}) collective-permute-start(bf16[128,512]{0,1:T(8,128)(2,1)S(1)} %get-tuple-element.383), channel_id=1, source_target_pairs={{0,32},{32,64},{64,96},{96,128},{128,160},{160,192},{192,224},{224... | collective-permute-start | bytes 393224 | tf_op jit(solution)/shard_map/while/body/eval_jaxpr/ppermute | solution.py:16
  131.0 11.0 %collective-permute-start.1 = (bf16[128,512]{0,1:T(8,128)(2,1)S(1)}, bf16[128,512]{0,1:T(8,128)(2,1)S(1)}, u32[]{:S(2)}, u32[]{:S(2)}) collective-permute-start(bf16[128,512]{0,1:T(8,128)(2,1)S(1)} %get-tuple-element.384), channel_id=1, source_target_pairs={{0,32},{32,64},{64,96},{96,128},{128,160},{160,192},{192,224},{224... | collective-permute-start | bytes 393224 | tf_op jit(solution)/shard_map/while/body/eval_jaxpr/ppermute | solution.py:16
  142.7 10.8 %collective-permute-start = (bf16[128,512]{0,1:T(8,128)(2,1)S(1)}, bf16[128,512]{0,1:T(8,128)(2,1)S(1)}, u32[]{:S(2)}, u32[]{:S(2)}) collective-permute-start(bf16[128,512]{0,1:T(8,128)(2,1)S(1)} %get-tuple-element.383), channel_id=1, source_target_pairs={{0,32},{32,64},{64,96},{96,128},{128,160},{160,192},{192,224},{224... | collective-permute-start | bytes 393224 | tf_op jit(solution)/shard_map/while/body/eval_jaxpr/ppermute | solution.py:16
  144.6 11.4 %collective-permute-start.1 = (bf16[128,512]{0,1:T(8,128)(2,1)S(1)}, bf16[128,512]{0,1:T(8,128)(2,1)S(1)}, u32[]{:S(2)}, u32[]{:S(2)}) collective-permute-start(bf16[128,512]{0,1:T(8,128)(2,1)S(1)} %get-tuple-element.384), channel_id=1, source_target_pairs={{0,32},{32,64},{64,96},{96,128},{128,160},{160,192},{192,224},{224... | collective-permute-start | bytes 393224 | tf_op jit(solution)/shard_map/while/body/eval_jaxpr/ppermute | solution.py:16
  156.7 10.3 %collective-permute-start = (bf16[128,512]{0,1:T(8,128)(2,1)S(1)}, bf16[128,512]{0,1:T(8,128)(2,1)S(1)}, u32[]{:S(2)}, u32[]{:S(2)}) collective-permute-start(bf16[128,512]{0,1:T(8,128)(2,1)S(1)} %get-tuple-element.383), channel_id=1, source_target_pairs={{0,32},{32,64},{64,96},{96,128},{128,160},{160,192},{192,224},{224... | collective-permute-start | bytes 393224 | tf_op jit(solution)/shard_map/while/body/eval_jaxpr/ppermute | solution.py:16
  158.7 10.4 %collective-permute-start.1 = (bf16[128,512]{0,1:T(8,128)(2,1)S(1)}, bf16[128,512]{0,1:T(8,128)(2,1)S(1)}, u32[]{:S(2)}, u32[]{:S(2)}) collective-permute-start(bf16[128,512]{0,1:T(8,128)(2,1)S(1)} %get-tuple-element.384), channel_id=1, source_target_pairs={{0,32},{32,64},{64,96},{96,128},{128,160},{160,192},{192,224},{224... | collective-permute-start | bytes 393224 | tf_op jit(solution)/shard_map/while/body/eval_jaxpr/ppermute | solution.py:16
  169.8 10.0 %collective-permute-start = (bf16[128,512]{0,1:T(8,128)(2,1)S(1)}, bf16[128,512]{0,1:T(8,128)(2,1)S(1)}, u32[]{:S(2)}, u32[]{:S(2)}) collective-permute-start(bf16[128,512]{0,1:T(8,128)(2,1)S(1)} %get-tuple-element.383), channel_id=1, source_target_pairs={{0,32},{32,64},{64,96},{96,128},{128,160},{160,192},{192,224},{224... | collective-permute-start | bytes 393224 | tf_op jit(solution)/shard_map/while/body/eval_jaxpr/ppermute | solution.py:16
  171.7 9.9 %collective-permute-start.1 = (bf16[128,512]{0,1:T(8,128)(2,1)S(1)}, bf16[128,512]{0,1:T(8,128)(2,1)S(1)}, u32[]{:S(2)}, u32[]{:S(2)}) collective-permute-start(bf16[128,512]{0,1:T(8,128)(2,1)S(1)} %get-tuple-element.384), channel_id=1, source_target_pairs={{0,32},{32,64},{64,96},{96,128},{128,160},{160,192},{192,224},{224... | collective-permute-start | bytes 393224 | tf_op jit(solution)/shard_map/while/body/eval_jaxpr/ppermute | solution.py:16
  194.9 11.3 %collective-permute-start = (bf16[128,512]{0,1:T(8,128)(2,1)S(1)}, bf16[128,512]{0,1:T(8,128)(2,1)S(1)}, u32[]{:S(2)}, u32[]{:S(2)}) collective-permute-start(bf16[128,512]{0,1:T(8,128)(2,1)S(1)} %get-tuple-element.383), channel_id=1, source_target_pairs={{0,32},{32,64},{64,96},{96,128},{128,160},{160,192},{192,224},{224... | collective-permute-start | bytes 393224 | tf_op jit(solution)/shard_map/while/body/eval_jaxpr/ppermute | solution.py:16
  196.8 11.7 %collective-permute-start.1 = (bf16[128,512]{0,1:T(8,128)(2,1)S(1)}, bf16[128,512]{0,1:T(8,128)(2,1)S(1)}, u32[]{:S(2)}, u32[]{:S(2)}) collective-permute-start(bf16[128,512]{0,1:T(8,128)(2,1)S(1)} %get-tuple-element.384), channel_id=1, source_target_pairs={{0,32},{32,64},{64,96},{96,128},{128,160},{160,192},{192,224},{224... | collective-permute-start | bytes 393224 | tf_op jit(solution)/shard_map/while/body/eval_jaxpr/ppermute | solution.py:16
  209.3 10.0 %collective-permute-start = (bf16[128,512]{0,1:T(8,128)(2,1)S(1)}, bf16[128,512]{0,1:T(8,128)(2,1)S(1)}, u32[]{:S(2)}, u32[]{:S(2)}) collective-permute-start(bf16[128,512]{0,1:T(8,128)(2,1)S(1)} %get-tuple-element.383), channel_id=1, source_target_pairs={{0,32},{32,64},{64,96},{96,128},{128,160},{160,192},{192,224},{224... | collective-permute-start | bytes 393224 | tf_op jit(solution)/shard_map/while/body/eval_jaxpr/ppermute | solution.py:16
  211.2 11.2 %collective-permute-start.1 = (bf16[128,512]{0,1:T(8,128)(2,1)S(1)}, bf16[128,512]{0,1:T(8,128)(2,1)S(1)}, u32[]{:S(2)}, u32[]{:S(2)}) collective-permute-start(bf16[128,512]{0,1:T(8,128)(2,1)S(1)} %get-tuple-element.384), channel_id=1, source_target_pairs={{0,32},{32,64},{64,96},{96,128},{128,160},{160,192},{192,224},{224... | collective-permute-start | bytes 393224 | tf_op jit(solution)/shard_map/while/body/eval_jaxpr/ppermute | solution.py:16
  223.2 10.9 %collective-permute-start = (bf16[128,512]{0,1:T(8,128)(2,1)S(1)}, bf16[128,512]{0,1:T(8,128)(2,1)S(1)}, u32[]{:S(2)}, u32[]{:S(2)}) collective-permute-start(bf16[128,512]{0,1:T(8,128)(2,1)S(1)} %get-tuple-element.383), channel_id=1, source_target_pairs={{0,32},{32,64},{64,96},{96,128},{128,160},{160,192},{192,224},{224... | collective-permute-start | bytes 393224 | tf_op jit(solution)/shard_map/while/body/eval_jaxpr/ppermute | solution.py:16
  225.1 11.0 %collective-permute-start.1 = (bf16[128,512]{0,1:T(8,128)(2,1)S(1)}, bf16[128,512]{0,1:T(8,128)(2,1)S(1)}, u32[]{:S(2)}, u32[]{:S(2)}) collective-permute-start(bf16[128,512]{0,1:T(8,128)(2,1)S(1)} %get-tuple-element.384), channel_id=1, source_target_pairs={{0,32},{32,64},{64,96},{96,128},{128,160},{160,192},{192,224},{224... | collective-permute-start | bytes 393224 | tf_op jit(solution)/shard_map/while/body/eval_jaxpr/ppermute | solution.py:16
  236.9 11.0 %collective-permute-start = (bf16[128,512]{0,1:T(8,128)(2,1)S(1)}, bf16[128,512]{0,1:T(8,128)(2,1)S(1)}, u32[]{:S(2)}, u32[]{:S(2)}) collective-permute-start(bf16[128,512]{0,1:T(8,128)(2,1)S(1)} %get-tuple-element.383), channel_id=1, source_target_pairs={{0,32},{32,64},{64,96},{96,128},{128,160},{160,192},{192,224},{224... | collective-permute-start | bytes 393224 | tf_op jit(solution)/shard_map/while/body/eval_jaxpr/ppermute | solution.py:16
  238.8 11.9 %collective-permute-start.1 = (bf16[128,512]{0,1:T(8,128)(2,1)S(1)}, bf16[128,512]{0,1:T(8,128)(2,1)S(1)}, u32[]{:S(2)}, u32[]{:S(2)}) collective-permute-start(bf16[128,512]{0,1:T(8,128)(2,1)S(1)} %get-tuple-element.384), channel_id=1, source_target_pairs={{0,32},{32,64},{64,96},{96,128},{128,160},{160,192},{192,224},{224... | collective-permute-start | bytes 393224 | tf_op jit(solution)/shard_map/while/body/eval_jaxpr/ppermute | solution.py:16
  251.4 10.9 %collective-permute-start = (bf16[128,512]{0,1:T(8,128)(2,1)S(1)}, bf16[128,512]{0,1:T(8,128)(2,1)S(1)}, u32[]{:S(2)}, u32[]{:S(2)}) collective-permute-start(bf16[128,512]{0,1:T(8,128)(2,1)S(1)} %get-tuple-element.383), channel_id=1, source_target_pairs={{0,32},{32,64},{64,96},{96,128},{128,160},{160,192},{192,224},{224... | collective-permute-start | bytes 393224 | tf_op jit(solution)/shard_map/while/body/eval_jaxpr/ppermute | solution.py:16
  253.3 11.7 %collective-permute-start.1 = (bf16[128,512]{0,1:T(8,128)(2,1)S(1)}, bf16[128,512]{0,1:T(8,128)(2,1)S(1)}, u32[]{:S(2)}, u32[]{:S(2)}) collective-permute-start(bf16[128,512]{0,1:T(8,128)(2,1)S(1)} %get-tuple-element.384), channel_id=1, source_target_pairs={{0,32},{32,64},{64,96},{96,128},{128,160},{160,192},{192,224},{224... | collective-permute-start | bytes 393224 | tf_op jit(solution)/shard_map/while/body/eval_jaxpr/ppermute | solution.py:16
  (10 other events, 386.9 us)
Sparse Core Ops, SparseCore 0:
  10.1 168.0 all-gather.4
  180.3 130.6 all-gather.2
  367.1 84.0 reduce-scatter.1
